TPU v7x, 256 devices: a whole 4x4x8 slice. The times are simulated.
256 devices in a mesh: row: 64 (over y, z, core), col: 4 (over x).
Axes of the slice: x: 4, y: 4, z: 8, core: 2. Of those that a mesh axis runs over, the one named last changes fastest.
Arguments:
- features: bfloat16 [65536, 256], P('row', 'col'), may hold values from -600 to 600
- tile_vals: bfloat16 [10240, 128, 128], P('row'), may hold values from -0.125 to 0.125
- tile_rows: int32 [64, 160], P('row'), may hold values from 0 to 7
- tile_srcs: int32 [64, 160], P('row'), may hold values from 0 to 135, as said below
- tile_count: int32 [64], P('row'), may hold values from 20 to 160, as said below
- needed: int32 [64, 64, 2], P('row'), may hold values from 0 to 7, as said below
- hop_noise: float32 [2, 65536, 256], P(None, 'row', 'col'), may hold values from -0.24 to 0.24
- enc_weight: bfloat16 [3, 256, 256], replicated, may hold values from -3.59375 to 3.59375
Outputs:
- encoded: bfloat16 [65536, 256], P('row', 'col')
Inputs may be any that keep to these rules, and one draw needn't show every extreme that they name: `tile_count`: some row index has exactly 160 live slots; slots at or beyond a row index's count are ignored. `tile_srcs`: A value s below 8 names the row index's own block s; otherwise s = 8 + o * 2 + c names entry c of needed for owner o, and o is never the row index itself. needed[d, o, :] are 2 distinct block indices among owner o's 8 blocks.
All inputs are finite; a program needn't handle non-finite values.
Results may differ from a plain program's by a relative error of at most 0.0053.
Values may be sent and summed in bfloat16 or wider, within the bound.
No kernel may reach another device: no remote copies, remote signals or barrier semaphores. Data moves between devices by JAX's collectives and lax.ppermute only.
A program may use at most 64 MiB of HBM per device.

v0:
```python
import jax
import jax.numpy as jnp
from jax import lax
from jax.sharding import PartitionSpec as P

BLK = 128
BPD = 8
TPD = 160
CAP = 2
HOPS = 2
epsilon = 1e-06


def shards(features, tile_vals, tile_rows, tile_srcs, tile_count, needed, hop_noise, enc_weight):
    row_count = lax.axis_size("row")
    row_index = lax.axis_index("row")
    col_index = lax.axis_index("col")
    local_rows, local_width = features.shape
    sources = tile_srcs[0]
    block_rows = tile_rows[0]
    live_count = tile_count[0]
    wanted = needed[0]
    tile_order = jnp.arange(TPD, dtype=jnp.int32)
    onehot = (
        (block_rows[:, None] == jnp.arange(BPD, dtype=jnp.int32)[None, :])
        & (tile_order < live_count)[:, None]
    ).astype(jnp.float32)

    def normalize(values):
        squares = lax.psum(jnp.sum(values * values, axis=1), "col")
        return (values / jnp.sqrt(squares + epsilon)[:, None]).astype(jnp.bfloat16)

    remote = jnp.maximum(sources - BPD, 0)
    slot_table = wanted.reshape(-1)
    looked_up = jnp.sum(
        jnp.where(
            remote[:, None] == jnp.arange(row_count * CAP, dtype=jnp.int32)[None, :],
            slot_table[None, :],
            0,
        ),
        axis=1,
    )
    global_block = jnp.where(
        sources < BPD, row_index * BPD + sources, remote // CAP * BPD + looked_up
    )
    current = normalize(features.astype(jnp.float32))
    layers = [current]
    for hop_index in range(HOPS):
        whole = lax.all_gather(current.reshape(BPD, BLK * local_width), "row", axis=0, tiled=True)
        products = jnp.einsum(
            "tij,tjf->tif",
            tile_vals,
            jnp.take(whole, global_block, axis=0).reshape(TPD, BLK, local_width),
            preferred_element_type=jnp.float32,
        )
        summed = jnp.einsum("tr,tif->rif", onehot, products, precision=lax.Precision.HIGHEST)
        current = normalize(summed.reshape(local_rows, local_width) + hop_noise[hop_index])
        layers.append(current)
    stacked = jnp.stack(layers)
    weight_slice = lax.dynamic_slice_in_dim(
        enc_weight, col_index * local_width, local_width, axis=1
    )
    terms = jnp.einsum("kri,kio->ro", stacked, weight_slice, preferred_element_type=jnp.float32)
    encoded = lax.psum_scatter(terms, "col", scatter_dimension=1, tiled=True)
    return encoded.astype(jnp.bfloat16)


def solution(mesh):
    in_specs = (
        P("row", "col"),
        P("row", None, None),
        P("row", None),
        P("row", None),
        P("row"),
        P("row", None, None),
        P(None, "row", "col"),
        P(),
    )
    out_specs = P("row", "col")
    return jax.shard_map(shards, mesh=mesh, in_specs=in_specs, out_specs=out_specs, check_vma=False)
```

profile of v0, /device:TPU:8, one launch (start us, length us, event | category | flops | bytes accessed | tf_op | source)
XLA Modules:
  0.0 299.7 jit_solution(14227140690207375910)
XLA Ops:
  6.5 0.0 copy-start
  6.5 0.0 all-gather.3.cloned.1.call-start
  6.5 1.0 fusion.9
  7.5 10.5 %psum.21 = f32[1024]{0:T(1024)S(1)} all-reduce(f32[1024]{0:T(1024)S(1)} %fusion.9), channel_id=1, replica_groups=mesh['row'=64,'col'=4] {'col'}, use_global_device_ids=true, to_apply=%region_1.2 | all-reduce | flops 1024 | bytes 8192 | tf_op jit(solution)/shard_map/psum | solution.py:30
  18.0 0.9 fusion.10
  19.0 0.2 copy.15
  19.2 0.9 reshape.66
  20.1 0.0 all-gather.3.cloned.1.call-update
  20.1 0.0 all-gather.5.cloned.1.call-start
  20.2 0.8 copy.14
  20.9 0.1 broadcast_in_dim.30
  21.7 1.0 slice_bitcast_fusion.1
  22.7 0.8 copy.24
  23.5 0.5 iota_compare_fusion.2
  24.0 0.7 compare_reduce_fusion
  24.7 0.7 add_maximum_fusion
  25.4 0.2 select_reduce_fusion
  25.6 77.1 %all-gather.3.cloned.1.call-done = bf16[512,8192]{1,0:T(8,128)(2,1)} async-done(((bf16[8,8192]{1,0:T(8,128)(2,1)}), bf16[512,8192]{1,0:T(8,128)(2,1)}) %all-gather.3.cloned.1.call-update) | async-done | bytes 8388624 | tf_op jit(solution)/shard_map/all_gather | solution.py:49
  102.7 9.0 %gather_fusion = bf16[160,8192]{1,0:T(8,128)(2,1)S(1)} fusion(bf16[512,8192]{1,0:T(8,128)(2,1)} %all-gather.3.cloned.1.call-done, s32[1024]{0:T(1024)S(1)} %pad_clamp_fusion), kind=kCustom, calls=%fused_computation.clone | custom fusion | bytes 5243520 | tf_op jit(solution)/shard_map/jit(_take)/gather | solution.py:53
  111.8 1.8 broadcast_select_fusion.1
  113.6 8.4 %reshape.67 = bf16[160,128,64]{2,1,0:T(8,128)(2,1)} reshape(bf16[160,8192]{1,0:T(8,128)(2,1)} %broadcast_select_fusion.1) | data formatting | bytes 5242880 | tf_op jit(solution)/shard_map/reshape | solution.py:53
  122.0 0.0 copy-start.3
  122.0 0.0 copy-start.7
  122.0 0.0 copy-start.8
  122.0 7.7 %convolution_bitcast_fusion.1 = f32[160,128,64]{1,2,0:T(8,128)S(1)} fusion(bf16[160,128,64]{2,1,0:T(8,128)(2,1)} %reshape.67, bf16[160,128,128]{2,1,0:T(8,128)(2,1)} %param.11), kind=kOutput, calls=%fused_computation.9 | convolution fusion | flops 335544320 | bytes 13107200 | tf_op jit(solution)/shard_map/tij,tjf->tif/dot_general | solution.py:50
  129.7 0.0 copy-start.1
  129.7 0.0 copy-done.3
  129.7 0.0 copy-done.7
  129.7 0.0 copy-done.8
  129.8 0.0 copy-start.2
  129.8 4.7 %fusion.14 = (f32[8,128]{1,0:T(8,128)S(1)}, f32[8,128,64]{1,0,2:T(8,128)S(1)}) fusion(f32[8,8,8,128]{3,2,1,0:T(8,128)S(1)} %copy-done.3, f32[160,128,64]{1,2,0:T(8,128)S(1)} %convolution_bitcast_fusion.1, s32[160]{0:T(256)S(1)} %bitcast.59, pred[160]{0:T(512)(128)(4,1)S(1)} %copy-done.8), kind=kOutput, calls=%fused_computation.25 | convolution fusion | flops 126027264 | bytes 5772064 | tf_op jit(solution)/shard_map/tr,tif->rif/dot_general | solution.py:56
  134.6 0.2 copy.18
  134.8 10.4 %psum.22 = f32[1024]{0:T(1024)S(1)} all-reduce(f32[1024]{0:T(1024)S(1)} %bitcast.55), channel_id=1, replica_groups=mesh['row'=64,'col'=4] {'col'}, use_global_device_ids=true, to_apply=%region_4.6 | all-reduce | flops 1024 | bytes 8192 | tf_op jit(solution)/shard_map/psum | solution.py:30
  145.2 0.0 copy-done.1
  145.2 0.7 divide_convert_fusion.2
  146.0 0.2 copy.19
  146.2 0.2 squeeze.14
  146.4 0.2 div.47
  146.6 0.2 div.48
  146.7 0.2 reshape.69
  146.9 0.7 divide_convert_fusion.1
  147.6 0.0 all-gather.5.cloned.1.call-update
  147.6 0.3 reduce-scatter.2.cloned.1.call-start
  147.9 0.0 copy-done.2
  147.9 0.7 fusion.31
  148.6 0.8 copy.25
  149.4 76.1 %all-gather.5.cloned.1.call-done = bf16[512,8192]{1,0:T(8,128)(2,1)} async-done(((bf16[8,8192]{1,0:T(8,128)(2,1)}), bf16[512,8192]{1,0:T(8,128)(2,1)}) %all-gather.5.cloned.1.call-update) | async-done | bytes 8388624 | tf_op jit(solution)/shard_map/all_gather | solution.py:49
  225.4 9.0 %gather_fusion.1 = bf16[160,8192]{1,0:T(8,128)(2,1)S(1)} fusion(bf16[512,8192]{1,0:T(8,128)(2,1)} %all-gather.5.cloned.1.call-done, s32[1024]{0:T(1024)S(1)} %pad_clamp_fusion), kind=kCustom, calls=%fused_computation.1.clone | custom fusion | bytes 5243520 | tf_op jit(solution)/shard_map/jit(_take)/gather | solution.py:53
  234.5 1.8 broadcast_select_fusion
  236.3 8.4 %reshape.70 = bf16[160,128,64]{2,1,0:T(8,128)(2,1)} reshape(bf16[160,8192]{1,0:T(8,128)(2,1)} %broadcast_select_fusion) | data formatting | bytes 5242880 | tf_op jit(solution)/shard_map/reshape | solution.py:53
  244.7 7.7 %convolution_bitcast_fusion = f32[160,128,64]{1,2,0:T(8,128)S(1)} fusion(bf16[160,128,64]{2,1,0:T(8,128)(2,1)} %reshape.70, bf16[160,128,128]{2,1,0:T(8,128)(2,1)} %param.11), kind=kOutput, calls=%fused_computation.8 | convolution fusion | flops 335544320 | bytes 13107200 | tf_op jit(solution)/shard_map/tij,tjf->tif/dot_general | solution.py:50
  252.4 0.0 copy-done.4
  252.4 0.0 copy-done.9
  252.4 0.0 copy-start.5
  252.4 0.0 copy-start.6
  252.5 4.7 %fusion.12 = (f32[8,128]{1,0:T(8,128)S(1)}, f32[8,128,64]{1,0,2:T(8,128)S(1)}) fusion(f32[8,8,8,128]{3,2,1,0:T(8,128)S(1)} %copy-done.4, f32[160,128,64]{1,2,0:T(8,128)S(1)} %convolution_bitcast_fusion, s32[160]{0:T(256)S(1)} %bitcast.60, pred[160]{0:T(512)(128)(4,1)S(1)} %copy-done.9), kind=kOutput, calls=%fused_computation.22 | convolution fusion | flops 126027264 | bytes 5772064 | tf_op jit(solution)/shard_map/tr,tif->rif/dot_general | solution.py:56
  257.3 10.4 %psum.23 = f32[1024]{0:T(1024)S(1)} all-reduce(f32[1024]{0:T(1024)S(1)} %bitcast.56), channel_id=1, replica_groups=mesh['row'=64,'col'=4] {'col'}, use_global_device_ids=true, to_apply=%region_6.8 | all-reduce | flops 1024 | bytes 8192 | tf_op jit(solution)/shard_map/psum | solution.py:30
  267.7 0.0 copy-done
  267.8 0.0 copy-done.5
  267.8 0.0 copy-done.6
  267.8 1.3 convolution_bitcast_fusion.2
  269.1 0.0 reduce-scatter.2.cloned.1.call-update
  269.1 22.4 %reduce-scatter.2.cloned.1.call-done = f32[1024,64]{0,1:T(8,128)} async-done(((f32[1024,256]{0,1:T(8,128)}), f32[1024,64]{0,1:T(8,128)}) %reduce-scatter.2.cloned.1.call-update) | async-done | bytes 262160 | tf_op jit(solution)/shard_map/reduce_scatter | solution.py:64
  291.5 1.6 convert_element_type.26
  (10 shorter events, 0.2 us)
Async XLA Ops:
  6.5 261.2 %copy-start = (bf16[3,256,256]{2,1,0:T(8,128)(2,1)S(1)}, bf16[3,256,256]{2,1,0:T(8,128)(2,1)}, u32[]{:S(2)}) copy-start(bf16[3,256,256]{2,1,0:T(8,128)(2,1)} %param.17) | copy-start | bytes 1179652
  6.5 96.2 %all-gather.3.cloned.1.call-start = ((), (), s32[]{:S(2)}) async-start(), calls=%async_computation.1 | async-start | bytes 8519680 | tf_op jit(solution)/shard_map/all_gather | solution.py:49
  20.1 205.3 %all-gather.5.cloned.1.call-start = ((), (), s32[]{:S(2)}) async-start(), calls=%async_computation.2 | async-start | bytes 8519680 | tf_op jit(solution)/shard_map/all_gather | solution.py:49
  122.0 7.7 %copy-start.3 = (f32[8,8,8,128]{3,2,1,0:T(8,128)S(1)}, f32[8,8,8,128]{3,2,1,0:T(8,128)}, u32[]{:S(2)}) copy-start(f32[8,8,8,128]{3,2,1,0:T(8,128)} %copy.24) | copy-start | bytes 786436
  122.0 7.7 %copy-start.7 = (s32[1,160]{1,0:T(1,128)S(1)}, s32[1,160]{1,0:T(1,128)}, u32[]{:S(2)}) copy-start(s32[1,160]{1,0:T(1,128)} %param.12) | copy-start | bytes 1924
  122.0 7.7 %copy-start.8 = (pred[160]{0:T(512)(128)(4,1)S(1)}, pred[160]{0:T(512)(128)(4,1)}, u32[]{:S(2)}) copy-start(pred[160]{0:T(512)(128)(4,1)} %iota_compare_fusion.2) | copy-start | bytes 484
  129.7 15.5 %copy-start.1 = (f32[2,1024,64]{1,2,0:T(8,128)S(1)}, f32[2,1024,64]{1,2,0:T(8,128)}, u32[]{:S(2)}) copy-start(f32[2,1024,64]{1,2,0:T(8,128)} %param.16) | copy-start | bytes 1572868
  129.8 18.2 %copy-start.2 = (bf16[1024,64]{0,1:T(8,128)(2,1)S(1)}, bf16[1024,64]{0,1:T(8,128)(2,1)}, u32[]{:S(2)}) copy-start(bf16[1024,64]{0,1:T(8,128)(2,1)} %param.10) | copy-start | bytes 393220
  147.6 143.9 %reduce-scatter.2.cloned.1.call-start = ((), (), s32[]{:S(2)}) async-start(), calls=%async_computation.3 | async-start | bytes 1310720 | tf_op jit(solution)/shard_map/reduce_scatter | solution.py:64
  244.7 7.7 %copy-start.4 = (f32[8,8,8,128]{3,2,1,0:T(8,128)S(1)}, f32[8,8,8,128]{3,2,1,0:T(8,128)}, u32[]{:S(2)}) copy-start(f32[8,8,8,128]{3,2,1,0:T(8,128)} %copy.25) | copy-start | bytes 786436
  244.7 7.7 %copy-start.9 = (pred[160]{0:T(512)(128)(4,1)S(1)}, pred[160]{0:T(512)(128)(4,1)}, u32[]{:S(2)}) copy-start(pred[160]{0:T(512)(128)(4,1)} %iota_compare_fusion.2) | copy-start | bytes 484
  252.4 15.3 %copy-start.5 = (bf16[1,1024,64]{1,2,0:T(8,128)(2,1)S(1)}, bf16[1,1024,64]{1,2,0:T(8,128)(2,1)}, u32[]{:S(2)}) copy-start(bf16[1,1024,64]{1,2,0:T(8,128)(2,1)} %fusion.31) | copy-start | bytes 393220
  252.4 15.3 %copy-start.6 = (bf16[1,1024,64]{1,2,0:T(8,128)(2,1)S(1)}, bf16[1,1024,64]{1,2,0:T(8,128)(2,1)}, u32[]{:S(2)}) copy-start(bf16[1,1024,64]{1,2,0:T(8,128)(2,1)} %get-tuple-element.8) | copy-start | bytes 393220
Sparse Core Ops, SparseCore 0:
  20.2 82.4 all-gather.2
  147.8 77.6 all-gather.4
  269.3 22.2 reduce-scatter.1
where the time goes:
time: 300 us
  waiting for transfers between devices  176 us (59%)
  local copies, waits for them, and re-layouts  40.7 us (14%)
  blocking collectives  31.4 us (10%)
  matrix products  26.2 us (9%)
  between operations  14 us (5%)
  other arithmetic  11.5 us (4%)
    all_gather x2, waiting for transfers between devices, shards(): lax.all_gather(current.reshape(BPD, BLK * local_width), 'row', axis=0, ti...  153 us
    psum x3, blocking collectives, normalize(): squares = lax.psum(jnp.sum(values * values, axis=1), 'col')  31.4 us
    reduce_scatter x1, waiting for transfers between devices, shards(): encoded = lax.psum_scatter(terms, 'col', scatter_dimension=1, tiled=True)  22.4 us
    gather x2, local copies, waits for them, and re-layouts, shards(): jnp.take(whole, global_block, axis=0).reshape(TPD, BLK, local_width)  18.1 us
    reshape x2, local copies, waits for them, and re-layouts, shards(): jnp.take(whole, global_block, axis=0).reshape(TPD, BLK, local_width)  16.8 us
    dot_general x2, matrix products, shards(): jnp.einsum('tij,tjf->tif', tile_vals, jnp.take(whole, global_block, axis=...  15.4 us
    dot_general x2, matrix products, shards(): jnp.einsum('tr,tif->rif', onehot, products, precision=lax.Precision.HIGHEST)  9.47 us
  transfers between devices with their start and end apart: 3, of which 3 were waited for; matrix products, arithmetic and copies ran while one was open for 2% of the time, Pallas kernels for 0%

commit v1 on v0

--- a/solution.py
+++ b/solution.py
@@ -46,7 +46,15 @@
     current = normalize(features.astype(jnp.float32))
     layers = [current]
     for hop_index in range(HOPS):
-        whole = lax.all_gather(current.reshape(BPD, BLK * local_width), "row", axis=0, tiled=True)
+        whole = jnp.concatenate(
+            lax.all_to_all(
+                jnp.stack(lax.axis_size("row") * [current.reshape(BPD, BLK * local_width)], 0),
+                "row",
+                0,
+                0,
+            ),
+            0,
+        )
         products = jnp.einsum(
             "tij,tjf->tif",
             tile_vals,

time: 300 us -> 532 us (1.77)
  waiting for transfers between devices: 176 us -> 387 us
  starting transfers between devices: 0.31 us -> 20.2 us
  local copies, waits for them, and re-layouts: 40.7 us -> 46.8 us
    all_to_all x0 -> x2, waiting for transfers between devices: none -> 364 us  [shards(): lax.all_to_all(jnp.stack(lax.axis_size('row') * [current.reshape(BPD, BLK...]
    all_gather x2 -> x0, waiting for transfers between devices: 153 us -> none  [shards(): lax.all_gather(current.reshape(BPD, BLK * local_width), 'row', axis=0, ti...]
    all_to_all x0 -> x2, starting transfers between devices: none -> 19.9 us  [shards(): lax.all_to_all(jnp.stack(lax.axis_size('row') * [current.reshape(BPD, BLK...]
    another operation x0 -> x3, local copies, waits for them, and re-layouts: none -> 8.73 us  [shards(): jnp.stack(lax.axis_size('row') * [current.reshape(BPD, BLK * local_width)...]
  transfers between devices with their start and end apart: 3 -> 3, of which waited for: 3 -> 3; matrix products, arithmetic and copies ran while one was open for 2% -> 1% of each run, Pallas kernels for 0% -> 0%
where the time goes in v1:
time: 532 us
  waiting for transfers between devices  387 us (73%)
  local copies, waits for them, and re-layouts  46.8 us (9%)
  blocking collectives  28 us (5%)
  matrix products  26.2 us (5%)
  starting transfers between devices  20.2 us (4%)
  between operations  14.3 us (3%)
  other arithmetic  9.51 us (2%)
    all_to_all x2, waiting for transfers between devices, shards(): lax.all_to_all(jnp.stack(lax.axis_size('row') * [current.reshape(BPD, BLK...  364 us
    psum x3, blocking collectives, normalize(): squares = lax.psum(jnp.sum(values * values, axis=1), 'col')  28 us
    reduce_scatter x1, waiting for transfers between devices, shards(): encoded = lax.psum_scatter(terms, 'col', scatter_dimension=1, tiled=True)  22.2 us
    all_to_all x2, starting transfers between devices, shards(): lax.all_to_all(jnp.stack(lax.axis_size('row') * [current.reshape(BPD, BLK...  19.9 us
    gather x2, local copies, waits for them, and re-layouts, shards(): jnp.take(whole, global_block, axis=0).reshape(TPD, BLK, local_width)  18.1 us
    reshape x2, local copies, waits for them, and re-layouts, shards(): jnp.take(whole, global_block, axis=0).reshape(TPD, BLK, local_width)  16.8 us
    dot_general x2, matrix products, shards(): jnp.einsum('tij,tjf->tif', tile_vals, jnp.take(whole, global_block, axis=...  15.4 us
  transfers between devices with their start and end apart: 3, of which 3 were waited for; matrix products, arithmetic and copies ran while one was open for 1% of the time, Pallas kernels for 0%

profile of v1, /device:TPU:8, one launch (start us, length us, event | category | flops | bytes accessed | tf_op | source)
XLA Modules:
  0.0 531.6 jit_solution(4693057574266179005)
XLA Ops:
  6.5 0.0 copy-start
  6.5 1.0 fusion.9
  7.5 10.5 %psum.21 = f32[1024]{0:T(1024)S(1)} all-reduce(f32[1024]{0:T(1024)S(1)} %fusion.9), channel_id=1, replica_groups=mesh['row'=64,'col'=4] {'col'}, use_global_device_ids=true, to_apply=%region_1.2 | all-reduce | flops 1024 | bytes 8192 | tf_op jit(solution)/shard_map/psum | solution.py:30
  18.0 0.9 fusion.10
  19.0 0.2 copy.15
  19.2 0.3 stack_reshape.2
  19.4 4.2 stack.15
  23.7 0.0 copy-start.10
  23.7 0.0 copy-start.1
  23.7 0.0 copy-start.11
  23.7 12.4 %all-to-all-start = ((bf16[64,8,8192]{2,1,0:T(8,128)(2,1)}), bf16[64,8,8192]{2,1,0:T(8,128)(2,1)}, u32[]{:S(2)}, u32[]{:S(2)}) async-start(bf16[64,8,8192]{2,1,0:T(8,128)(2,1)} %stack.15), calls=%async_computation | async-start | bytes 16777216 | tf_op jit(solution)/shard_map/all_to_all | solution.py:50
  36.1 0.0 copy-done.10
  36.1 0.1 copy.14
  36.2 0.1 broadcast_in_dim.30
  37.0 0.0 copy-done.1
  37.0 0.7 copy.24
  37.8 0.5 iota_compare_fusion.2
  38.3 0.0 copy-done.11
  38.4 0.2 select_reduce_fusion
  38.6 181.8 %all-to-all-done = bf16[64,8,8192]{2,1,0:T(8,128)(2,1)} async-done(((bf16[64,8,8192]{2,1,0:T(8,128)(2,1)}), bf16[64,8,8192]{2,1,0:T(8,128)(2,1)}, u32[]{:S(2)}, u32[]{:S(2)}) %all-to-all-start) | async-done | bytes 8388640 | tf_op jit(solution)/shard_map/all_to_all | solution.py:50
  220.3 9.0 %gather_fusion = bf16[160,8192]{1,0:T(8,128)(2,1)S(1)} fusion(bf16[512,8192]{1,0:T(8,128)(2,1)} %bitcast.6, s32[1024]{0:T(1024)S(1)} %pad_clamp_fusion), kind=kCustom, calls=%fused_computation.clone | custom fusion | bytes 5243520 | tf_op jit(solution)/shard_map/jit(_take)/gather | solution.py:61
  229.4 1.8 broadcast_select_fusion.1
  231.2 8.4 %reshape.78 = bf16[160,128,64]{2,1,0:T(8,128)(2,1)} reshape(bf16[160,8192]{1,0:T(8,128)(2,1)} %broadcast_select_fusion.1) | data formatting | bytes 5242880 | tf_op jit(solution)/shard_map/reshape | solution.py:61
  239.6 0.0 copy-start.3
  239.6 0.0 copy-start.7
  239.6 0.0 copy-start.8
  239.6 7.7 %convolution_bitcast_fusion.1 = f32[160,128,64]{1,2,0:T(8,128)S(1)} fusion(bf16[160,128,64]{2,1,0:T(8,128)(2,1)} %reshape.78, bf16[160,128,128]{2,1,0:T(8,128)(2,1)} %param.11), kind=kOutput, calls=%fused_computation.9 | convolution fusion | flops 335544320 | bytes 13107200 | tf_op jit(solution)/shard_map/tij,tjf->tif/dot_general | solution.py:58
  247.3 0.0 copy-done.3
  247.3 0.0 copy-done.7
  247.3 0.0 copy-done.8
  247.4 4.7 fusion.14
  252.1 0.2 copy.18
  252.4 7.8 %psum.22 = f32[1024]{0:T(1024)S(1)} all-reduce(f32[1024]{0:T(1024)S(1)} %bitcast.57), channel_id=1, replica_groups=mesh['row'=64,'col'=4] {'col'}, use_global_device_ids=true, to_apply=%region_4.6 | all-reduce | flops 1024 | bytes 8192 | tf_op jit(solution)/shard_map/psum | solution.py:30
  260.1 0.7 divide_convert_fusion.2
  260.9 0.2 copy.19
  261.1 0.2 squeeze.14
  261.3 0.2 div.48
  261.5 0.2 div.49
  261.6 0.2 reshape.80
  261.9 4.2 stack.16
  266.1 0.0 copy-start.2
  266.1 7.5 %all-to-all-start.1 = ((bf16[64,8,8192]{2,1,0:T(8,128)(2,1)}), bf16[64,8,8192]{2,1,0:T(8,128)(2,1)}, u32[]{:S(2)}, u32[]{:S(2)}) async-start(bf16[64,8,8192]{2,1,0:T(8,128)(2,1)} %stack.16), calls=%async_computation.1 | async-start | bytes 16777216 | tf_op jit(solution)/shard_map/all_to_all | solution.py:50
  273.6 0.3 reduce-scatter.2.cloned.1.call-start
  273.9 0.0 copy-done.2
  273.9 0.7 fusion.31
  274.6 0.7 copy.25
  275.3 182.5 %all-to-all-done.1 = bf16[64,8,8192]{2,1,0:T(8,128)(2,1)} async-done(((bf16[64,8,8192]{2,1,0:T(8,128)(2,1)}), bf16[64,8,8192]{2,1,0:T(8,128)(2,1)}, u32[]{:S(2)}, u32[]{:S(2)}) %all-to-all-start.1) | async-done | bytes 8388640 | tf_op jit(solution)/shard_map/all_to_all | solution.py:50
  457.9 9.0 %gather_fusion.1 = bf16[160,8192]{1,0:T(8,128)(2,1)S(1)} fusion(bf16[512,8192]{1,0:T(8,128)(2,1)} %bitcast.10, s32[1024]{0:T(1024)S(1)} %pad_clamp_fusion), kind=kCustom, calls=%fused_computation.1.clone | custom fusion | bytes 5243520 | tf_op jit(solution)/shard_map/jit(_take)/gather | solution.py:61
  466.9 1.8 broadcast_select_fusion
  468.7 8.4 %reshape.82 = bf16[160,128,64]{2,1,0:T(8,128)(2,1)} reshape(bf16[160,8192]{1,0:T(8,128)(2,1)} %broadcast_select_fusion) | data formatting | bytes 5242880 | tf_op jit(solution)/shard_map/reshape | solution.py:61
  477.1 7.7 %convolution_bitcast_fusion = f32[160,128,64]{1,2,0:T(8,128)S(1)} fusion(bf16[160,128,64]{2,1,0:T(8,128)(2,1)} %reshape.82, bf16[160,128,128]{2,1,0:T(8,128)(2,1)} %param.11), kind=kOutput, calls=%fused_computation.8 | convolution fusion | flops 335544320 | bytes 13107200 | tf_op jit(solution)/shard_map/tij,tjf->tif/dot_general | solution.py:58
  484.8 0.0 copy-done.4
  484.9 0.0 copy-done.9
  484.9 0.0 copy-start.5
  484.9 0.0 copy-start.6
  484.9 4.7 fusion.12
  489.7 9.8 %psum.23 = f32[1024]{0:T(1024)S(1)} all-reduce(f32[1024]{0:T(1024)S(1)} %bitcast.58), channel_id=1, replica_groups=mesh['row'=64,'col'=4] {'col'}, use_global_device_ids=true, to_apply=%region_6.8 | all-reduce | flops 1024 | bytes 8192 | tf_op jit(solution)/shard_map/psum | solution.py:30
  499.5 0.0 copy-done
  499.5 0.0 copy-done.5
  499.5 0.0 copy-done.6
  499.5 1.3 convolution_bitcast_fusion.2
  500.9 0.0 reduce-scatter.2.cloned.1.call-update
  500.9 22.2 %reduce-scatter.2.cloned.1.call-done = f32[1024,64]{0,1:T(8,128)} async-done(((f32[1024,256]{0,1:T(8,128)}), f32[1024,64]{0,1:T(8,128)}) %reduce-scatter.2.cloned.1.call-update) | async-done | bytes 262160 | tf_op jit(solution)/shard_map/reduce_scatter | solution.py:72
  523.1 1.6 convert_element_type.27
  (14 shorter events, 0.3 us)
Async XLA Ops:
  6.5 493.0 %copy-start = (bf16[3,256,256]{2,1,0:T(8,128)(2,1)S(1)}, bf16[3,256,256]{2,1,0:T(8,128)(2,1)}, u32[]{:S(2)}) copy-start(bf16[3,256,256]{2,1,0:T(8,128)(2,1)} %param.17) | copy-start | bytes 1179652
  23.7 12.5 %copy-start.10 = (s32[1,64,2]{1,2,0:T(2,128)S(1)}, s32[1,64,2]{1,2,0:T(2,128)}, u32[]{:S(2)}) copy-start(s32[1,64,2]{1,2,0:T(2,128)} %param.15) | copy-start | bytes 1540
  23.7 13.4 %copy-start.1 = (f32[2,1024,64]{1,2,0:T(8,128)S(1)}, f32[2,1024,64]{1,2,0:T(8,128)}, u32[]{:S(2)}) copy-start(f32[2,1024,64]{1,2,0:T(8,128)} %param.16) | copy-start | bytes 1572868
  23.7 14.7 %copy-start.11 = (s32[1,160]{1,0:T(1,128)S(1)}, s32[1,160]{1,0:T(1,128)}, u32[]{:S(2)}) copy-start(s32[1,160]{1,0:T(1,128)} %param.13) | copy-start | bytes 1924
  23.7 196.7 %all-to-all-start = ((bf16[64,8,8192]{2,1,0:T(8,128)(2,1)}), bf16[64,8,8192]{2,1,0:T(8,128)(2,1)}, u32[]{:S(2)}, u32[]{:S(2)}) async-start(bf16[64,8,8192]{2,1,0:T(8,128)(2,1)} %stack.15), calls=%async_computation | async-start | bytes 16777216 | tf_op jit(solution)/shard_map/all_to_all | solution.py:50
  239.6 7.7 %copy-start.3 = (f32[8,8,8,128]{3,2,1,0:T(8,128)S(1)}, f32[8,8,8,128]{3,2,1,0:T(8,128)}, u32[]{:S(2)}) copy-start(f32[8,8,8,128]{3,2,1,0:T(8,128)} %copy.24) | copy-start | bytes 786436
  239.6 7.7 %copy-start.7 = (s32[1,160]{1,0:T(1,128)S(1)}, s32[1,160]{1,0:T(1,128)}, u32[]{:S(2)}) copy-start(s32[1,160]{1,0:T(1,128)} %param.12) | copy-start | bytes 1924
  239.6 7.7 %copy-start.8 = (pred[160]{0:T(512)(128)(4,1)S(1)}, pred[160]{0:T(512)(128)(4,1)}, u32[]{:S(2)}) copy-start(pred[160]{0:T(512)(128)(4,1)} %iota_compare_fusion.2) | copy-start | bytes 484
  266.1 7.8 %copy-start.2 = (bf16[1024,64]{0,1:T(8,128)(2,1)S(1)}, bf16[1024,64]{0,1:T(8,128)(2,1)}, u32[]{:S(2)}) copy-start(bf16[1024,64]{0,1:T(8,128)(2,1)} %param.10) | copy-start | bytes 393220
  266.1 191.8 %all-to-all-start.1 = ((bf16[64,8,8192]{2,1,0:T(8,128)(2,1)}), bf16[64,8,8192]{2,1,0:T(8,128)(2,1)}, u32[]{:S(2)}, u32[]{:S(2)}) async-start(bf16[64,8,8192]{2,1,0:T(8,128)(2,1)} %stack.16), calls=%async_computation.1 | async-start | bytes 16777216 | tf_op jit(solution)/shard_map/all_to_all | solution.py:50
  273.6 249.5 %reduce-scatter.2.cloned.1.call-start = ((), (), s32[]{:S(2)}) async-start(), calls=%async_computation.3 | async-start | bytes 1310720 | tf_op jit(solution)/shard_map/reduce_scatter | solution.py:72
  477.1 7.7 %copy-start.4 = (f32[8,8,8,128]{3,2,1,0:T(8,128)S(1)}, f32[8,8,8,128]{3,2,1,0:T(8,128)}, u32[]{:S(2)}) copy-start(f32[8,8,8,128]{3,2,1,0:T(8,128)} %copy.25) | copy-start | bytes 786436
  477.1 7.7 %copy-start.9 = (pred[160]{0:T(512)(128)(4,1)S(1)}, pred[160]{0:T(512)(128)(4,1)}, u32[]{:S(2)}) copy-start(pred[160]{0:T(512)(128)(4,1)} %iota_compare_fusion.2) | copy-start | bytes 484
  484.9 14.6 %copy-start.5 = (bf16[1,1024,64]{1,2,0:T(8,128)(2,1)S(1)}, bf16[1,1024,64]{1,2,0:T(8,128)(2,1)}, u32[]{:S(2)}) copy-start(bf16[1,1024,64]{1,2,0:T(8,128)(2,1)} %fusion.31) | copy-start | bytes 393220
  484.9 14.6 %copy-start.6 = (bf16[1,1024,64]{1,2,0:T(8,128)(2,1)S(1)}, bf16[1,1024,64]{1,2,0:T(8,128)(2,1)}, u32[]{:S(2)}) copy-start(bf16[1,1024,64]{1,2,0:T(8,128)(2,1)} %get-tuple-element.8) | copy-start | bytes 393220
Sparse Core Ops, SparseCore 0:
  501.0 22.0 reduce-scatter.1
